TPU v7x, 32 devices: a whole 2x2x4 slice. The times are simulated.
32 devices in a mesh: sample: 4 (over x, core), space: 8 (over z, y).
Axes of the slice: x: 2, y: 2, z: 4, core: 2. Of those that a mesh axis runs over, the one named last changes fastest.
Arguments:
- acts: bfloat16 [8, 8, 16, 8, 8, 128], P('sample', 'space'), may hold values from -6 to 6
- weight: float32 [3456, 128], P('space'), may hold values from -0.109375 to 0.109375
- moment: float32 [3456, 128], P('space'), may hold values from -3 to 3
- second: float32 [3456, 128], P('space'), may hold values from 0.05 to 2
- cotangent: bfloat16 [8, 8, 16, 8, 8, 128], P('sample', 'space'), may hold values from -6 to 6
Outputs:
- output: bfloat16 [8, 8, 16, 8, 8, 128], P('sample', 'space')
- input_grad: bfloat16 [8, 8, 16, 8, 8, 128], P('sample', 'space')
- weight_grad: float32 [3456, 128], P('space')
- new_weight: float32 [3456, 128], P('space')
- new_moment: float32 [3456, 128], P('space')
- new_second: float32 [3456, 128], P('space')
All inputs are finite; a program needn't handle non-finite values.
Results may differ from a plain program's by a relative error of at most 0.0062.
Values may be sent and summed in bfloat16 or wider, within the bound.
A program may use at most 64 MiB of HBM per device.

v0:
```python
import jax
import jax.numpy as jnp
from jax import lax
from jax.sharding import PartitionSpec as P

GY = 2
GZ = 4
root_coef = 0.7978845608
cubic_coef = 0.044715


def shifted(value, axis, by):
    devices = lax.axis_size(axis)
    pairs = [(i, i + by) for i in range(devices) if 0 <= i + by < devices]
    return lax.ppermute(value, axis, pairs)


def convolve(field, kernel):
    return lax.conv_general_dilated(
        field,
        kernel,
        (1, 1, 1),
        "VALID",
        dimension_numbers=("NDHWC", "DHWIO", "NDHWC"),
        preferred_element_type=jnp.float32,
    )


def activate(pre):
    inner = root_coef * (pre + cubic_coef * pre * pre * pre)
    tval = jnp.tanh(inner)
    value = 0.5 * pre * (1.0 + tval)
    slope = 0.5 * (1.0 + tval) + 0.5 * pre * (1.0 - tval * tval) * root_coef * (
        1.0 + 3.0 * cubic_coef * pre * pre
    )
    return (value, slope)


def extend(field):
    place = lax.axis_index("space")
    groups = lax.axis_size("space") // (GY * GZ)
    coord_z = place % GZ
    coord_y = place // GZ % GY
    coord_x = place // (GZ * GY)
    for dim, stride, coord, count in (
        (3, 1, coord_z, GZ),
        (2, GZ, coord_y, GY),
        (1, GY * GZ, coord_x, groups),
    ):
        length = field.shape[dim]
        first_layer = lax.slice_in_dim(field, 0, 1, 1, dim)
        last_layer = lax.slice_in_dim(field, length - 1, length, 1, dim)
        below = shifted(last_layer, "space", stride)
        above = shifted(first_layer, "space", -stride)
        below = jnp.where(coord > 0, below, jnp.zeros_like(below))
        above = jnp.where(coord < count - 1, above, jnp.zeros_like(above))
        field = jnp.concatenate([below, field, above], dim)
    return field


def kernel_terms(padded, grad_pre):
    nx, ny, nz = (grad_pre.shape[1], grad_pre.shape[2], grad_pre.shape[3])
    terms = []
    for kx in range(3):
        for ky in range(3):
            for kz in range(3):
                window = padded[:, kx : kx + nx, ky : ky + ny, kz : kz + nz, :]
                terms.append(
                    lax.dot_general(
                        window,
                        grad_pre,
                        (((0, 1, 2, 3), (0, 1, 2, 3)), ((), ())),
                        preferred_element_type=jnp.float32,
                    )
                )
    stacked = jnp.stack(terms, 0)
    return stacked.reshape(27 * stacked.shape[1], stacked.shape[2])


def local(acts, weight, moment, second, cotangent):
    field = acts[:, 0]
    grad_out = cotangent[:, 0]
    channels = weight.shape[1]
    rows_bf = weight.astype(jnp.bfloat16)
    whole = lax.all_gather(rows_bf, "space", axis=0, tiled=True)
    kernel = whole.reshape(3, 3, 3, channels, channels)
    padded = extend(field)
    pre = convolve(padded, kernel)
    value, slope = activate(pre)
    output = value.astype(jnp.bfloat16)
    grad_pre = (grad_out.astype(jnp.float32) * slope).astype(jnp.bfloat16)
    flipped = jnp.flip(kernel, (0, 1, 2)).transpose(0, 1, 2, 4, 3)
    grad_padded = extend(grad_pre)
    input_grad = convolve(grad_padded, flipped).astype(jnp.bfloat16)
    total = (
        field.shape[0]
        * lax.axis_size("sample")
        * lax.axis_size("space")
        * field.shape[1]
        * field.shape[2]
        * field.shape[3]
    )
    local_terms = kernel_terms(padded, grad_pre) * float(total) ** (-0.5)
    owned = lax.psum_scatter(local_terms, "space", scatter_dimension=0, tiled=True)
    weight_grad = lax.psum(owned, "sample")
    new_moment = 0.9 * moment + 0.1 * weight_grad
    new_second = 0.999 * second + 0.001 * weight_grad * weight_grad
    first_fix = 1.0 - 0.9**10
    second_fix = 1.0 - 0.999**10
    new_weight = weight - 0.001 * (new_moment / first_fix) / (
        jnp.sqrt(new_second / second_fix) + 1e-08
    )
    return (output[:, None], input_grad[:, None], weight_grad, new_weight, new_moment, new_second)


def solution(mesh):
    in_specs = (
        P("sample", "space", None, None, None, None),
        P("space", None),
        P("space", None),
        P("space", None),
        P("sample", "space", None, None, None, None),
    )
    out_specs = (
        P("sample", "space", None, None, None, None),
        P("sample", "space", None, None, None, None),
        P("space", None),
        P("space", None),
        P("space", None),
        P("space", None),
    )
    return jax.shard_map(local, mesh=mesh, in_specs=in_specs, out_specs=out_specs, check_vma=False)
```

profile of v0, /device:TPU:0, one launch (start us, length us, event | category | flops | bytes accessed | tf_op | source)
XLA Modules:
  0.0 203.3 jit_solution(16130695142617238557)
XLA Ops:
  7.2 1.5 fusion.71
  8.7 1.3 collective-permute-start.1
  10.0 5.5 %collective-permute-start = (bf16[2,16,8,1,128]{4,3,2,1,0:T(2,128)(2,1)S(1)}, bf16[2,16,8,1,128]{4,3,2,1,0:T(2,128)(2,1)S(1)}, u32[]{:S(2)}, u32[]{:S(2)}) collective-permute-start(bf16[2,16,8,1,128]{4,3,2,1,0:T(2,128)(2,1)S(1)} %get-tuple-element.37), channel_id=1, source_target_pairs={{0,1},{1,2},{2,3},{3,4},{4,5},{5,6},{6,7},{8,9},{9,10},{10,11},{11... | collective-permute-start | bytes 196616 | tf_op jit(solution)/shard_map/ppermute | solution.py:15
  17.2 2.8 %collective-permute-done = bf16[2,16,8,1,128]{4,3,2,1,0:T(2,128)(2,1)S(1)} collective-permute-done((bf16[2,16,8,1,128]{4,3,2,1,0:T(2,128)(2,1)S(1)}, bf16[2,16,8,1,128]{4,3,2,1,0:T(2,128)(2,1)S(1)}, u32[]{:S(2)}, u32[]{:S(2)}) %collective-permute-start) | collective-permute-done | bytes 65568 | tf_op jit(solution)/shard_map/ppermute | solution.py:15
  20.4 1.3 collective-permute-start.3
  21.7 35.9 %all_gather.3 = bf16[3456,128]{1,0:T(8,128)(2,1)S(1)} all-gather(bf16[432,128]{1,0:T(8,128)(2,1)S(1)} %convert_element_type.18), channel_id=1, replica_groups=mesh['sample'=4,'space'=8] {'space'}, dimensions={0}, use_global_device_ids=true | all-gather | bytes 995328 | tf_op jit(solution)/shard_map/all_gather | solution.py:85
  57.6 1.3 collective-permute-start.2
  58.9 2.5 %collective-permute-done.2 = bf16[2,16,1,10,128]{4,3,2,1,0:T(8,128)(2,1)S(1)} collective-permute-done((bf16[2,16,1,10,128]{4,3,2,1,0:T(8,128)(2,1)S(1)}, bf16[2,16,1,10,128]{4,3,2,1,0:T(8,128)(2,1)S(1)}, u32[]{:S(2)}, u32[]{:S(2)}) %collective-permute-start.2) | collective-permute-done | bytes 81952 | tf_op jit(solution)/shard_map/ppermute | solution.py:15
  62.1 1.4 pad_maximum_fusion.3
  65.0 1.5 pad_maximum_fusion.2
  66.6 6.3 %fusion.36 = f32[2,16,8,8,128]{4,0,3,2,1:T(2,128)S(1)} fusion(bf16[3,3,3,128,128]{4,3,2,1,0:T(8,128)(2,1)S(1)} %bitcast.272, bf16[2,18,10,10,128]{4,3,2,1,0:T(8,128)(2,1)S(1)} %pad_maximum_fusion), kind=kOutput, calls=%fused_computation.73 | convolution fusion | flops 1811939328 | bytes 2854912 | tf_op jit(solution)/shard_map/conv_general_dilated | solution.py:19
  72.9 1.6 fusion.34
  84.6 1.4 broadcast_multiply_fusion
  86.3 1.3 collective-permute-start.7
  87.6 4.6 %collective-permute-start.6 = (bf16[2,16,8,1,128]{4,3,2,1,0:T(2,128)(2,1)S(1)}, bf16[2,16,8,1,128]{4,3,2,1,0:T(2,128)(2,1)S(1)}, u32[]{:S(2)}, u32[]{:S(2)}) collective-permute-start(bf16[2,16,8,1,128]{4,3,2,1,0:T(2,128)(2,1)S(1)} %get-tuple-element.35), channel_id=1, source_target_pairs={{0,1},{1,2},{2,3},{3,4},{4,5},{5,6},{6,7},{8,9},{9,10},{10,11},{11... | collective-permute-start | bytes 196616 | tf_op jit(solution)/shard_map/ppermute | solution.py:15
  93.3 1.3 collective-permute-done.6
  95.0 1.3 collective-permute-start.9
  96.3 18.0 %collective-permute-start.8 = (bf16[2,16,1,10,128]{4,3,2,1,0:T(8,128)(2,1)S(1)}, bf16[2,16,1,10,128]{4,3,2,1,0:T(8,128)(2,1)S(1)}, u32[]{:S(2)}, u32[]{:S(2)}) collective-permute-start(bf16[2,16,1,10,128]{4,3,2,1,0:T(8,128)(2,1)S(1)} %get-tuple-element.31), channel_id=1, source_target_pairs={{0,4},{1,5},{2,6},{3,7},{8,12},{9,13},{10,14},{11,15},{16,20},{17,... | collective-permute-start | bytes 245768 | tf_op jit(solution)/shard_map/ppermute | solution.py:15
  114.3 3.2 %collective-permute-done.9 = bf16[2,16,1,10,128]{4,3,2,1,0:T(8,128)(2,1)S(1)} collective-permute-done((bf16[2,16,1,10,128]{4,3,2,1,0:T(8,128)(2,1)S(1)}, bf16[2,16,1,10,128]{4,3,2,1,0:T(8,128)(2,1)S(1)}, u32[]{:S(2)}, u32[]{:S(2)}) %collective-permute-start.9) | collective-permute-done | bytes 81952 | tf_op jit(solution)/shard_map/ppermute | solution.py:15
  120.2 39.6 %reduce-scatter.2.cloned.1.call-done = f32[432,128]{1,0:T(8,128)} async-done(((f32[3456,128]{1,0:T(8,128)}), f32[432,128]{1,0:T(8,128)}) %reduce-scatter.2.cloned.1.call-update) | async-done | bytes 221200 | tf_op jit(solution)/shard_map/reduce_scatter | solution.py:104
  159.9 7.3 %fusion = bf16[2,1,16,8,8,128]{5,0,4,3,2,1:T(2,128)(2,1)S(1)} fusion(bf16[3,3,3,128,128]{4,3,2,1,0:T(8,128)(2,1)} %bitcast.273, bf16[2,18,10,10,128]{4,3,2,1,0:T(8,128)(2,1)S(1)} %pad_maximum_fusion.1), kind=kOutput, calls=%fused_computation.7 | convolution fusion | flops 1812201472 | bytes 2330624 | tf_op jit(solution)/shard_map/conv_general_dilated | solution.py:19
  168.1 24.8 %all-reduce.2.cloned.1.call-done = f32[432,128]{1,0:T(8,128)} async-done(((f32[432,128]{1,0:T(8,128)}), f32[432,128]{1,0:T(8,128)}) %all-reduce.2.cloned.1.call-update) | async-done | bytes 221200 | tf_op jit(solution)/shard_map/psum | solution.py:105
  192.9 1.8 divide_subtract_fusion
  194.8 1.6 copy.256
  (76 shorter events, 19.6 us)
Async XLA Ops:
  7.2 13.0 %copy-start = (bf16[2,1,16,8,8,128]{5,4,3,2,1,0:T(8,128)(2,1)S(1)}, bf16[2,1,16,8,8,128]{5,4,3,2,1,0:T(8,128)(2,1)}, u32[]{:S(2)}) copy-start(bf16[2,1,16,8,8,128]{5,4,3,2,1,0:T(8,128)(2,1)} %param.5) | copy-start | bytes 1572868
  7.2 152.7 %reduce-scatter.2.cloned.1.call-start = ((), (), s32[]{:S(2)}) async-start(), calls=%async_computation.1 | async-start | bytes 1990656 | tf_op jit(solution)/shard_map/reduce_scatter | solution.py:104
  8.7 8.4 %collective-permute-start.1 = (bf16[2,16,8,1,128]{4,3,2,1,0:T(2,128)(2,1)S(1)}, bf16[2,16,8,1,128]{4,3,2,1,0:T(2,128)(2,1)S(1)}, u32[]{:S(2)}, u32[]{:S(2)}) collective-permute-start(bf16[2,16,8,1,128]{4,3,2,1,0:T(2,128)(2,1)S(1)} %get-tuple-element.38), channel_id=1, source_target_pairs={{1,0},{2,1},{3,2},{4,3},{5,4},{6,5},{7,6},{9,8},{10,9},{11,10},{12... | collective-permute-start | bytes 196616 | tf_op jit(solution)/shard_map/ppermute | solution.py:15
  10.0 10.1 %collective-permute-start = (bf16[2,16,8,1,128]{4,3,2,1,0:T(2,128)(2,1)S(1)}, bf16[2,16,8,1,128]{4,3,2,1,0:T(2,128)(2,1)S(1)}, u32[]{:S(2)}, u32[]{:S(2)}) collective-permute-start(bf16[2,16,8,1,128]{4,3,2,1,0:T(2,128)(2,1)S(1)} %get-tuple-element.37), channel_id=1, source_target_pairs={{0,1},{1,2},{2,3},{3,4},{4,5},{5,6},{6,7},{8,9},{9,10},{10,11},{11... | collective-permute-start | bytes 196616 | tf_op jit(solution)/shard_map/ppermute | solution.py:15
  20.4 38.5 %collective-permute-start.3 = (bf16[2,16,1,10,128]{4,3,2,1,0:T(8,128)(2,1)S(1)}, bf16[2,16,1,10,128]{4,3,2,1,0:T(8,128)(2,1)S(1)}, u32[]{:S(2)}, u32[]{:S(2)}) collective-permute-start(bf16[2,16,1,10,128]{4,3,2,1,0:T(8,128)(2,1)S(1)} %get-tuple-element.34), channel_id=1, source_target_pairs={{4,0},{5,1},{6,2},{7,3},{12,8},{13,9},{14,10},{15,11},{20,16},{21,... | collective-permute-start | bytes 245768 | tf_op jit(solution)/shard_map/ppermute | solution.py:15
  57.6 9.0 %copy-start.2 = (bf16[3456,128]{1,0:T(8,128)(2,1)}, bf16[3456,128]{1,0:T(8,128)(2,1)S(1)}, u32[]{:S(2)}) copy-start(bf16[3456,128]{1,0:T(8,128)(2,1)S(1)} %all_gather.3) | copy-start | bytes 2654212
  57.6 3.8 %collective-permute-start.2 = (bf16[2,16,1,10,128]{4,3,2,1,0:T(8,128)(2,1)S(1)}, bf16[2,16,1,10,128]{4,3,2,1,0:T(8,128)(2,1)S(1)}, u32[]{:S(2)}, u32[]{:S(2)}) collective-permute-start(bf16[2,16,1,10,128]{4,3,2,1,0:T(8,128)(2,1)S(1)} %get-tuple-element.33), channel_id=1, source_target_pairs={{0,4},{1,5},{2,6},{3,7},{8,12},{9,13},{10,14},{11,15},{16,20},{17,... | collective-permute-start | bytes 245768 | tf_op jit(solution)/shard_map/ppermute | solution.py:15
  61.5 2.7 %collective-permute-start.5 = (bf16[2,1,10,10,128]{4,3,2,1,0:T(8,128)(2,1)S(1)}, bf16[2,1,10,10,128]{4,3,2,1,0:T(8,128)(2,1)S(1)}, u32[]{:S(2)}, u32[]{:S(2)}) collective-permute-start(bf16[2,1,10,10,128]{4,3,2,1,0:T(8,128)(2,1)S(1)} %get-tuple-element.28), channel_id=1, source_target_pairs={} | collective-permute-start | bytes 153608 | tf_op jit(solution)/shard_map/ppermute | solution.py:15
  63.5 0.7 collective-permute-start.4
  66.5 6.3 %copy-start.3 = (bf16[2,1,16,8,8,128]{5,4,3,2,1,0:T(8,128)(2,1)S(1)}, bf16[2,1,16,8,8,128]{5,4,3,2,1,0:T(8,128)(2,1)}, u32[]{:S(2)}) copy-start(bf16[2,1,16,8,8,128]{5,4,3,2,1,0:T(8,128)(2,1)} %param.9) | copy-start | bytes 1572868
  86.1 106.9 %all-reduce.2.cloned.1.call-start = ((), (), s32[]{:S(2)}) async-start(), calls=%async_computation.2 | async-start | bytes 442368 | tf_op jit(solution)/shard_map/psum | solution.py:105
  86.3 6.9 %collective-permute-start.7 = (bf16[2,16,8,1,128]{4,3,2,1,0:T(2,128)(2,1)S(1)}, bf16[2,16,8,1,128]{4,3,2,1,0:T(2,128)(2,1)S(1)}, u32[]{:S(2)}, u32[]{:S(2)}) collective-permute-start(bf16[2,16,8,1,128]{4,3,2,1,0:T(2,128)(2,1)S(1)} %get-tuple-element.36), channel_id=1, source_target_pairs={{1,0},{2,1},{3,2},{4,3},{5,4},{6,5},{7,6},{9,8},{10,9},{11,10},{12... | collective-permute-start | bytes 196616 | tf_op jit(solution)/shard_map/ppermute | solution.py:15
  87.6 7.1 %collective-permute-start.6 = (bf16[2,16,8,1,128]{4,3,2,1,0:T(2,128)(2,1)S(1)}, bf16[2,16,8,1,128]{4,3,2,1,0:T(2,128)(2,1)S(1)}, u32[]{:S(2)}, u32[]{:S(2)}) collective-permute-start(bf16[2,16,8,1,128]{4,3,2,1,0:T(2,128)(2,1)S(1)} %get-tuple-element.35), channel_id=1, source_target_pairs={{0,1},{1,2},{2,3},{3,4},{4,5},{5,6},{6,7},{8,9},{9,10},{10,11},{11... | collective-permute-start | bytes 196616 | tf_op jit(solution)/shard_map/ppermute | solution.py:15
  95.0 22.5 %collective-permute-start.9 = (bf16[2,16,1,10,128]{4,3,2,1,0:T(8,128)(2,1)S(1)}, bf16[2,16,1,10,128]{4,3,2,1,0:T(8,128)(2,1)S(1)}, u32[]{:S(2)}, u32[]{:S(2)}) collective-permute-start(bf16[2,16,1,10,128]{4,3,2,1,0:T(8,128)(2,1)S(1)} %get-tuple-element.32), channel_id=1, source_target_pairs={{4,0},{5,1},{6,2},{7,3},{12,8},{13,9},{14,10},{15,11},{20,16},{21,... | collective-permute-start | bytes 245768 | tf_op jit(solution)/shard_map/ppermute | solution.py:15
  96.3 21.5 %collective-permute-start.8 = (bf16[2,16,1,10,128]{4,3,2,1,0:T(8,128)(2,1)S(1)}, bf16[2,16,1,10,128]{4,3,2,1,0:T(8,128)(2,1)S(1)}, u32[]{:S(2)}, u32[]{:S(2)}) collective-permute-start(bf16[2,16,1,10,128]{4,3,2,1,0:T(8,128)(2,1)S(1)} %get-tuple-element.31), channel_id=1, source_target_pairs={{0,4},{1,5},{2,6},{3,7},{8,12},{9,13},{10,14},{11,15},{16,20},{17,... | collective-permute-start | bytes 245768 | tf_op jit(solution)/shard_map/ppermute | solution.py:15
  117.9 1.6 collective-permute-start.11
  118.5 0.9 collective-permute-start.10
  159.9 33.1 %copy-start.1 = (f32[432,128]{1,0:T(8,128)S(1)}, f32[432,128]{1,0:T(8,128)}, u32[]{:S(2)}) copy-start(f32[432,128]{1,0:T(8,128)} %param.6) | copy-start | bytes 663556
  159.9 33.1 %copy-start.4 = (f32[432,128]{1,0:T(8,128)S(1)}, f32[432,128]{1,0:T(8,128)}, u32[]{:S(2)}) copy-start(f32[432,128]{1,0:T(8,128)} %param.7) | copy-start | bytes 663556
  159.9 33.1 %copy-start.5 = (f32[432,128]{1,0:T(8,128)S(1)}, f32[432,128]{1,0:T(8,128)}, u32[]{:S(2)}) copy-start(f32[432,128]{1,0:T(8,128)} %param.8) | copy-start | bytes 663556
Sparse Core Ops, SparseCore 0:
  86.2 73.5 reduce-scatter.1
  162.2 30.7 all-reduce.1
where the time goes:
time: 204 us; the launch traced here: 203 us
  waiting for transfers between devices  76.2 us (37%)
  starting transfers between devices  37.5 us (18%)
  blocking collectives  35.9 us (18%)
  matrix products  23.6 us (12%)
  between operations  14.5 us (7%)
  other arithmetic  11.4 us (6%)
  local copies, waits for them, and re-layouts  4.21 us (2%)
    reduce_scatter x1, waiting for transfers between devices, local(): lax.psum_scatter(local_terms, 'space', scatter_dimension=0, tiled=True)  39.6 us
    ppermute x12, starting transfers between devices, shifted(): return lax.ppermute(value, axis, pairs)  37.4 us
    all_gather x1, blocking collectives, local(): whole = lax.all_gather(rows_bf, 'space', axis=0, tiled=True)  35.9 us
    psum x1, waiting for transfers between devices, local(): weight_grad = lax.psum(owned, 'sample')  24.8 us
    conv_general_dilated x2, matrix products, convolve(): lax.conv_general_dilated(field, kernel, (1, 1, 1), 'VALID', dimension_num...  13.5 us
    ppermute x12, waiting for transfers between devices, shifted(): return lax.ppermute(value, axis, pairs)  11.7 us
    dot_general x27, matrix products, kernel_terms(): lax.dot_general(window, grad_pre, (((0, 1, 2, 3), (0, 1, 2, 3)), ((), ())...  10.1 us
    concatenate x4, other arithmetic, extend(): field = jnp.concatenate([below, field, above], dim)  4.4 us
  transfers between devices with their start and end apart: 14, of which 9 were waited for; matrix products, arithmetic and copies ran while one was open for 6% of the time, Pallas kernels for 0%

commit v1 on v0

--- a/solution.py
+++ b/solution.py
@@ -102,7 +102,7 @@
     )
     local_terms = kernel_terms(padded, grad_pre) * float(total) ** (-0.5)
     owned = lax.psum_scatter(local_terms, "space", scatter_dimension=0, tiled=True)
-    weight_grad = lax.psum(owned, "sample")
+    weight_grad = jnp.sum(lax.all_gather(owned, "sample"), axis=0)
     new_moment = 0.9 * moment + 0.1 * weight_grad
     new_second = 0.999 * second + 0.001 * weight_grad * weight_grad
     first_fix = 1.0 - 0.9**10

time: 204 us -> 178 us (0.87)
  waiting for transfers between devices: 76.2 us -> 44.3 us
  blocking collectives: 35.9 us -> 45.3 us
    psum x1 -> x0, waiting for transfers between devices: 24.8 us -> none  [local(): weight_grad = lax.psum(owned, 'sample')]
    all_gather x0 -> x1, blocking collectives: none -> 9.32 us  [local(): weight_grad = jnp.sum(lax.all_gather(owned, 'sample'), axis=0)]
    reduce_scatter x1, waiting for transfers between devices: 39.6 us -> 32.3 us  [local(): lax.psum_scatter(local_terms, 'space', scatter_dimension=0, tiled=True)]
  transfers between devices with their start and end apart: 14 -> 13, of which waited for: 9 -> 8; matrix products, arithmetic and copies ran while one was open for 6% -> 6% of each run, Pallas kernels for 0% -> 0%
where the time goes in v1:
time: 178 us; the launch traced here: 177 us
  blocking collectives  45.3 us (25%)
  waiting for transfers between devices  44.3 us (25%)
  starting transfers between devices  37.4 us (21%)
  matrix products  22.5 us (13%)
  between operations  14.5 us (8%)
  other arithmetic  10.5 us (6%)
  local copies, waits for them, and re-layouts  2.64 us (1%)
    ppermute x12, starting transfers between devices, shifted(): return lax.ppermute(value, axis, pairs)  37.4 us
    all_gather x1, blocking collectives, local(): whole = lax.all_gather(rows_bf, 'space', axis=0, tiled=True)  35.9 us
    reduce_scatter x1, waiting for transfers between devices, local(): lax.psum_scatter(local_terms, 'space', scatter_dimension=0, tiled=True)  32.3 us
    conv_general_dilated x2, matrix products, convolve(): lax.conv_general_dilated(field, kernel, (1, 1, 1), 'VALID', dimension_num...  12.5 us
    ppermute x12, waiting for transfers between devices, shifted(): return lax.ppermute(value, axis, pairs)  12 us
    dot_general x27, matrix products, kernel_terms(): lax.dot_general(window, grad_pre, (((0, 1, 2, 3), (0, 1, 2, 3)), ((), ())...  10.1 us
    all_gather x1, blocking collectives, local(): weight_grad = jnp.sum(lax.all_gather(owned, 'sample'), axis=0)  9.32 us
    concatenate x4, other arithmetic, extend(): field = jnp.concatenate([below, field, above], dim)  4.4 us
  transfers between devices with their start and end apart: 13, of which 8 were waited for; matrix products, arithmetic and copies ran while one was open for 6% of the time, Pallas kernels for 0%

profile of v1, /device:TPU:0, one launch (start us, length us, event | category | flops | bytes accessed | tf_op | source)
XLA Modules:
  0.0 177.2 jit_solution(913169068227492812)
XLA Ops:
  7.2 1.5 fusion.71
  8.7 1.3 collective-permute-start.1
  10.0 5.5 %collective-permute-start = (bf16[2,16,8,1,128]{4,3,2,1,0:T(2,128)(2,1)S(1)}, bf16[2,16,8,1,128]{4,3,2,1,0:T(2,128)(2,1)S(1)}, u32[]{:S(2)}, u32[]{:S(2)}) collective-permute-start(bf16[2,16,8,1,128]{4,3,2,1,0:T(2,128)(2,1)S(1)} %get-tuple-element.37), channel_id=1, source_target_pairs={{0,1},{1,2},{2,3},{3,4},{4,5},{5,6},{6,7},{8,9},{9,10},{10,11},{11... | collective-permute-start | bytes 196616 | tf_op jit(solution)/shard_map/ppermute | solution.py:15
  15.6 1.0 convert_element_type.18
  17.3 2.8 %collective-permute-done = bf16[2,16,8,1,128]{4,3,2,1,0:T(2,128)(2,1)S(1)} collective-permute-done((bf16[2,16,8,1,128]{4,3,2,1,0:T(2,128)(2,1)S(1)}, bf16[2,16,8,1,128]{4,3,2,1,0:T(2,128)(2,1)S(1)}, u32[]{:S(2)}, u32[]{:S(2)}) %collective-permute-start) | collective-permute-done | bytes 65568 | tf_op jit(solution)/shard_map/ppermute | solution.py:15
  20.4 1.3 collective-permute-start.3
  21.7 35.9 %all_gather.9 = bf16[3456,128]{1,0:T(8,128)(2,1)S(1)} all-gather(bf16[432,128]{1,0:T(8,128)(2,1)S(1)} %convert_element_type.18), channel_id=1, replica_groups=mesh['sample'=4,'space'=8] {'space'}, dimensions={0}, use_global_device_ids=true | all-gather | bytes 995328 | tf_op jit(solution)/shard_map/all_gather | solution.py:85
  57.6 1.3 collective-permute-start.2
  59.0 2.5 %collective-permute-done.2 = bf16[2,16,1,10,128]{4,3,2,1,0:T(8,128)(2,1)S(1)} collective-permute-done((bf16[2,16,1,10,128]{4,3,2,1,0:T(8,128)(2,1)S(1)}, bf16[2,16,1,10,128]{4,3,2,1,0:T(8,128)(2,1)S(1)}, u32[]{:S(2)}, u32[]{:S(2)}) %collective-permute-start.2) | collective-permute-done | bytes 81952 | tf_op jit(solution)/shard_map/ppermute | solution.py:15
  62.2 1.4 pad_maximum_fusion.3
  65.0 1.5 pad_maximum_fusion.2
  66.6 6.3 %fusion.36 = f32[2,16,8,8,128]{4,0,3,2,1:T(2,128)S(1)} fusion(bf16[3,3,3,128,128]{4,3,2,1,0:T(8,128)(2,1)S(1)} %bitcast.274, bf16[2,18,10,10,128]{4,3,2,1,0:T(8,128)(2,1)S(1)} %pad_maximum_fusion), kind=kOutput, calls=%fused_computation.73 | convolution fusion | flops 1811939328 | bytes 2854912 | tf_op jit(solution)/shard_map/conv_general_dilated | solution.py:19
  72.9 1.6 fusion.34
  84.7 1.4 broadcast_multiply_fusion
  86.3 1.3 collective-permute-start.7
  87.6 4.6 %collective-permute-start.6 = (bf16[2,16,8,1,128]{4,3,2,1,0:T(2,128)(2,1)S(1)}, bf16[2,16,8,1,128]{4,3,2,1,0:T(2,128)(2,1)S(1)}, u32[]{:S(2)}, u32[]{:S(2)}) collective-permute-start(bf16[2,16,8,1,128]{4,3,2,1,0:T(2,128)(2,1)S(1)} %get-tuple-element.35), channel_id=1, source_target_pairs={{0,1},{1,2},{2,3},{3,4},{4,5},{5,6},{6,7},{8,9},{9,10},{10,11},{11... | collective-permute-start | bytes 196616 | tf_op jit(solution)/shard_map/ppermute | solution.py:15
  92.2 1.0 collective-permute-done.7
  93.3 1.3 collective-permute-done.6
  95.0 1.3 collective-permute-start.9
  96.3 18.0 %collective-permute-start.8 = (bf16[2,16,1,10,128]{4,3,2,1,0:T(8,128)(2,1)S(1)}, bf16[2,16,1,10,128]{4,3,2,1,0:T(8,128)(2,1)S(1)}, u32[]{:S(2)}, u32[]{:S(2)}) collective-permute-start(bf16[2,16,1,10,128]{4,3,2,1,0:T(8,128)(2,1)S(1)} %get-tuple-element.31), channel_id=1, source_target_pairs={{0,4},{1,5},{2,6},{3,7},{8,12},{9,13},{10,14},{11,15},{16,20},{17,... | collective-permute-start | bytes 245768 | tf_op jit(solution)/shard_map/ppermute | solution.py:15
  114.3 3.3 %collective-permute-done.9 = bf16[2,16,1,10,128]{4,3,2,1,0:T(8,128)(2,1)S(1)} collective-permute-done((bf16[2,16,1,10,128]{4,3,2,1,0:T(8,128)(2,1)S(1)}, bf16[2,16,1,10,128]{4,3,2,1,0:T(8,128)(2,1)S(1)}, u32[]{:S(2)}, u32[]{:S(2)}) %collective-permute-start.9) | collective-permute-done | bytes 81952 | tf_op jit(solution)/shard_map/ppermute | solution.py:15
  120.5 6.2 %fusion = bf16[2,1,16,8,8,128]{5,0,4,3,2,1:T(2,128)(2,1)S(1)} fusion(bf16[3,3,3,128,128]{4,3,2,1,0:T(8,128)(2,1)S(1)} %bitcast.275, bf16[2,18,10,10,128]{4,3,2,1,0:T(8,128)(2,1)S(1)} %pad_maximum_fusion.1), kind=kOutput, calls=%fused_computation.7 | convolution fusion | flops 1812201472 | bytes 2330624 | tf_op jit(solution)/shard_map/conv_general_dilated | solution.py:19
  127.7 32.3 %reduce-scatter.2.cloned.1.call-done = f32[432,128]{1,0:T(8,128)} async-done(((f32[3456,128]{1,0:T(8,128)}), f32[432,128]{1,0:T(8,128)}) %reduce-scatter.2.cloned.1.call-update) | async-done | bytes 221200 | tf_op jit(solution)/shard_map/reduce_scatter | solution.py:104
  160.0 9.3 %all-gather = f32[1728,128]{1,0:T(8,128)S(1)} all-gather(f32[432,128]{1,0:T(8,128)} %reduce-scatter.2.cloned.1.call-done), channel_id=2, replica_groups=mesh['sample'=4,'space'=8] {'sample'}, dimensions={0}, use_global_device_ids=true | all-gather | bytes 1105920 | tf_op jit(solution)/shard_map/all_gather | solution.py:105
  (74 shorter events, 18.8 us)
Async XLA Ops:
  7.2 13.1 %copy-start = (bf16[2,1,16,8,8,128]{5,4,3,2,1,0:T(8,128)(2,1)S(1)}, bf16[2,1,16,8,8,128]{5,4,3,2,1,0:T(8,128)(2,1)}, u32[]{:S(2)}) copy-start(bf16[2,1,16,8,8,128]{5,4,3,2,1,0:T(8,128)(2,1)} %param.5) | copy-start | bytes 1572868
  7.2 152.8 %reduce-scatter.2.cloned.1.call-start = ((), (), s32[]{:S(2)}) async-start(), calls=%async_computation.1 | async-start | bytes 1990656 | tf_op jit(solution)/shard_map/reduce_scatter | solution.py:104
  8.7 8.4 %collective-permute-start.1 = (bf16[2,16,8,1,128]{4,3,2,1,0:T(2,128)(2,1)S(1)}, bf16[2,16,8,1,128]{4,3,2,1,0:T(2,128)(2,1)S(1)}, u32[]{:S(2)}, u32[]{:S(2)}) collective-permute-start(bf16[2,16,8,1,128]{4,3,2,1,0:T(2,128)(2,1)S(1)} %get-tuple-element.38), channel_id=1, source_target_pairs={{1,0},{2,1},{3,2},{4,3},{5,4},{6,5},{7,6},{9,8},{10,9},{11,10},{12... | collective-permute-start | bytes 196616 | tf_op jit(solution)/shard_map/ppermute | solution.py:15
  10.0 10.1 %collective-permute-start = (bf16[2,16,8,1,128]{4,3,2,1,0:T(2,128)(2,1)S(1)}, bf16[2,16,8,1,128]{4,3,2,1,0:T(2,128)(2,1)S(1)}, u32[]{:S(2)}, u32[]{:S(2)}) collective-permute-start(bf16[2,16,8,1,128]{4,3,2,1,0:T(2,128)(2,1)S(1)} %get-tuple-element.37), channel_id=1, source_target_pairs={{0,1},{1,2},{2,3},{3,4},{4,5},{5,6},{6,7},{8,9},{9,10},{10,11},{11... | collective-permute-start | bytes 196616 | tf_op jit(solution)/shard_map/ppermute | solution.py:15
  20.4 38.5 %collective-permute-start.3 = (bf16[2,16,1,10,128]{4,3,2,1,0:T(8,128)(2,1)S(1)}, bf16[2,16,1,10,128]{4,3,2,1,0:T(8,128)(2,1)S(1)}, u32[]{:S(2)}, u32[]{:S(2)}) collective-permute-start(bf16[2,16,1,10,128]{4,3,2,1,0:T(8,128)(2,1)S(1)} %get-tuple-element.34), channel_id=1, source_target_pairs={{4,0},{5,1},{6,2},{7,3},{12,8},{13,9},{14,10},{15,11},{20,16},{21,... | collective-permute-start | bytes 245768 | tf_op jit(solution)/shard_map/ppermute | solution.py:15
  57.6 3.8 %collective-permute-start.2 = (bf16[2,16,1,10,128]{4,3,2,1,0:T(8,128)(2,1)S(1)}, bf16[2,16,1,10,128]{4,3,2,1,0:T(8,128)(2,1)S(1)}, u32[]{:S(2)}, u32[]{:S(2)}) collective-permute-start(bf16[2,16,1,10,128]{4,3,2,1,0:T(8,128)(2,1)S(1)} %get-tuple-element.33), channel_id=1, source_target_pairs={{0,4},{1,5},{2,6},{3,7},{8,12},{9,13},{10,14},{11,15},{16,20},{17,... | collective-permute-start | bytes 245768 | tf_op jit(solution)/shard_map/ppermute | solution.py:15
  61.5 2.7 %collective-permute-start.5 = (bf16[2,1,10,10,128]{4,3,2,1,0:T(8,128)(2,1)S(1)}, bf16[2,1,10,10,128]{4,3,2,1,0:T(8,128)(2,1)S(1)}, u32[]{:S(2)}, u32[]{:S(2)}) collective-permute-start(bf16[2,1,10,10,128]{4,3,2,1,0:T(8,128)(2,1)S(1)} %get-tuple-element.28), channel_id=1, source_target_pairs={} | collective-permute-start | bytes 153608 | tf_op jit(solution)/shard_map/ppermute | solution.py:15
  63.6 0.7 collective-permute-start.4
  66.6 6.3 %copy-start.3 = (bf16[2,1,16,8,8,128]{5,4,3,2,1,0:T(8,128)(2,1)S(1)}, bf16[2,1,16,8,8,128]{5,4,3,2,1,0:T(8,128)(2,1)}, u32[]{:S(2)}) copy-start(bf16[2,1,16,8,8,128]{5,4,3,2,1,0:T(8,128)(2,1)} %param.9) | copy-start | bytes 1572868
  86.3 6.9 %collective-permute-start.7 = (bf16[2,16,8,1,128]{4,3,2,1,0:T(2,128)(2,1)S(1)}, bf16[2,16,8,1,128]{4,3,2,1,0:T(2,128)(2,1)S(1)}, u32[]{:S(2)}, u32[]{:S(2)}) collective-permute-start(bf16[2,16,8,1,128]{4,3,2,1,0:T(2,128)(2,1)S(1)} %get-tuple-element.36), channel_id=1, source_target_pairs={{1,0},{2,1},{3,2},{4,3},{5,4},{6,5},{7,6},{9,8},{10,9},{11,10},{12... | collective-permute-start | bytes 196616 | tf_op jit(solution)/shard_map/ppermute | solution.py:15
  87.6 7.1 %collective-permute-start.6 = (bf16[2,16,8,1,128]{4,3,2,1,0:T(2,128)(2,1)S(1)}, bf16[2,16,8,1,128]{4,3,2,1,0:T(2,128)(2,1)S(1)}, u32[]{:S(2)}, u32[]{:S(2)}) collective-permute-start(bf16[2,16,8,1,128]{4,3,2,1,0:T(2,128)(2,1)S(1)} %get-tuple-element.35), channel_id=1, source_target_pairs={{0,1},{1,2},{2,3},{3,4},{4,5},{5,6},{6,7},{8,9},{9,10},{10,11},{11... | collective-permute-start | bytes 196616 | tf_op jit(solution)/shard_map/ppermute | solution.py:15
  95.0 22.6 %collective-permute-start.9 = (bf16[2,16,1,10,128]{4,3,2,1,0:T(8,128)(2,1)S(1)}, bf16[2,16,1,10,128]{4,3,2,1,0:T(8,128)(2,1)S(1)}, u32[]{:S(2)}, u32[]{:S(2)}) collective-permute-start(bf16[2,16,1,10,128]{4,3,2,1,0:T(8,128)(2,1)S(1)} %get-tuple-element.32), channel_id=1, source_target_pairs={{4,0},{5,1},{6,2},{7,3},{12,8},{13,9},{14,10},{15,11},{20,16},{21,... | collective-permute-start | bytes 245768 | tf_op jit(solution)/shard_map/ppermute | solution.py:15
  96.3 21.8 %collective-permute-start.8 = (bf16[2,16,1,10,128]{4,3,2,1,0:T(8,128)(2,1)S(1)}, bf16[2,16,1,10,128]{4,3,2,1,0:T(8,128)(2,1)S(1)}, u32[]{:S(2)}, u32[]{:S(2)}) collective-permute-start(bf16[2,16,1,10,128]{4,3,2,1,0:T(8,128)(2,1)S(1)} %get-tuple-element.31), channel_id=1, source_target_pairs={{0,4},{1,5},{2,6},{3,7},{8,12},{9,13},{10,14},{11,15},{16,20},{17,... | collective-permute-start | bytes 245768 | tf_op jit(solution)/shard_map/ppermute | solution.py:15
  118.2 1.6 collective-permute-start.11
  118.8 0.9 collective-permute-start.10
  126.7 42.7 %copy-start.1 = (f32[432,128]{1,0:T(8,128)S(1)}, f32[432,128]{1,0:T(8,128)}, u32[]{:S(2)}) copy-start(f32[432,128]{1,0:T(8,128)} %param.6) | copy-start | bytes 663556
  126.7 42.7 %copy-start.4 = (f32[432,128]{1,0:T(8,128)S(1)}, f32[432,128]{1,0:T(8,128)}, u32[]{:S(2)}) copy-start(f32[432,128]{1,0:T(8,128)} %param.7) | copy-start | bytes 663556
  126.7 42.7 %copy-start.5 = (f32[432,128]{1,0:T(8,128)S(1)}, f32[432,128]{1,0:T(8,128)}, u32[]{:S(2)}) copy-start(f32[432,128]{1,0:T(8,128)} %param.8) | copy-start | bytes 663556
  169.4 0.9 copy-start.2
Sparse Core Ops, SparseCore 0:
  86.3 73.6 reduce-scatter.1
